TPU v7x, 32 devices: a whole 2x2x4 slice. The times are simulated.
32 devices in a mesh: obs: 4 (over y, x), bfly: 8 (over z, core).
Axes of the slice: x: 2, y: 2, z: 4, core: 2. Of those that a mesh axis runs over, the one named last changes fastest.
Arguments:
- obs_field: float32 [32768, 1024], P(('obs', 'bfly')), may hold values from -6 to 6
- observer_leaf_bases: float32 [64, 512, 256], P(('obs', 'bfly')), may hold values from -0.25 to 0.25
- transfer: float32 [3, 64, 256, 512], P(None, ('obs', 'bfly')), may hold values from -0.25 to 0.25
- src_basis: float32 [16, 512, 256], P('bfly'), may hold values from -0.375 to 0.375
- leaf_map: int32 [4, 8], replicated, may hold values from 0 to 3, as said below
- partner_perm: int32 [3, 256], replicated, may hold values from 0 to 255, each once within a row
Outputs:
- src_field: float32 [1024, 8192], P('obs', 'bfly')
Inputs may be any that keep to these rules, and one draw needn't show every extreme that they name: In every column b, leaf_map[o, b] = (o + r_b) mod 4 for one offset r_b of that column, so each column names every observer group once. `partner_perm`: each row is a permutation of the rank indices.
All inputs are finite; a program needn't handle non-finite values.
Results may differ from a plain program's by a relative error of at most 0.0001.
Values sent between devices are 32-bit elements; how exact they have to be, the bound alone decides.
A program may use at most 64 MiB of HBM per device.

v0:
```python
import functools

import jax
import jax.numpy as jnp
from jax import lax
from jax.experimental import pallas as pl
from jax.experimental.pallas import tpu as pltpu
from jax.sharding import PartitionSpec as P

MESH = pl.DeviceIdType.MESH
EXACT = lax.Precision.HIGHEST


def mm(a, b, rhs_dim=0):
    return lax.dot_general(
        a,
        b,
        (((1,), (rhs_dim,)), ((), ())),
        precision=EXACT,
        preferred_element_type=jnp.float32,
    )


def flip(index, bits):
    out = index
    for shift in range(3):
        unit = 1 << shift
        out = out + unit * ((bits // unit) % 2) * (1 - 2 * ((index // unit) % 2))
    return out


def kernel(
    groups,
    obs_ref,
    bases_ref,
    transfer_ref,
    src_ref,
    perm_ref,
    map_ref,
    out_ref,
    turned,
    far,
    far_away,
    send_a,
    send_b,
    cur,
    got,
    send_r,
    got_r,
    send_f,
    got_f,
    sem_w,
    sem_a,
    sem_b,
    sem_x,
    sem_r,
    sem_f,
    *arrived,
):
    nodes, leaf, rank = bases_ref.shape
    levels = transfer_ref.shape[0]
    last = levels - 1
    share = obs_ref.shape[1] // groups
    me = lax.axis_index("obs")
    col = lax.axis_index("bfly")

    def over_obs(k):
        return (flip(me, k), col)

    def over_bfly(level):
        unit = 1 << level
        return (me, col + unit * (1 - 2 * ((col // unit) % 2)))

    def remote(src, dst, sems, index, device):
        return pltpu.make_async_remote_copy(
            src_ref=src,
            dst_ref=dst,
            send_sem=sems.at[(0, *index)],
            recv_sem=sems.at[(1, *index)],
            device_id=device,
            device_id_type=MESH,
        )

    def copy_a(j, k):
        return remote(send_a.at[j, k], arrived[j].at[me], sem_a, (j, k), over_obs(k))

    def copy_b(j, k):
        return remote(send_b.at[j, k], cur.at[0, j, k], sem_b, (j, k), over_obs(k))

    def copy_x(level, j, k):
        return remote(
            cur.at[level, j, k], got.at[level, j, k], sem_x, (level, j, k), over_bfly(level)
        )

    def copy_r(which, j, k):
        return remote(
            send_r.at[which, j, k], got_r.at[which, j, k], sem_r, (which, j, k), over_obs(k)
        )

    def copy_f(j):
        return remote(send_f.at[j], got_f.at[j], sem_f, (j,), over_bfly(last))

    copy_w = remote(far.at[last], far_away, sem_w, (0,), over_bfly(last))

    barrier = pltpu.get_barrier_semaphore()
    for k in range(1, groups):
        pl.semaphore_signal(barrier, inc=1, device_id=over_obs(k), device_id_type=MESH)
    for level in range(levels):
        pl.semaphore_signal(barrier, inc=1, device_id=over_bfly(level), device_id_type=MESH)
    pl.semaphore_wait(barrier, groups - 1 + levels)

    for j in range(nodes):
        turned[j] = bases_ref[j].T

    def project(j, step, carry):
        k = groups - 1 - step
        first = pl.multiple_of(flip(me, k) * share, share)
        piece = obs_ref[j * leaf : (j + 1) * leaf, pl.ds(first, share)]
        value = mm(turned[j], piece)

        @pl.when(k > 0)
        def _():
            send_a[j, k] = value
            copy_a(j, k).start()

        @pl.when(k == 0)
        def _():
            arrived[j][me] = value

        return carry

    for j in range(nodes):
        lax.fori_loop(0, groups, functools.partial(project, j), 0)

    def fold(step, carry):
        level = last - step // nodes
        j = step % nodes
        hot = lax.broadcasted_iota(jnp.int32, (rank, rank), 0) == perm_ref[level]
        far[level, j] = mm(transfer_ref[level, j, :, rank:], hot.astype(jnp.float32), 1)

        @pl.when(step == nodes - 1)
        def _():
            copy_w.start()

        return carry

    lax.fori_loop(0, levels * nodes, fold, 0)

    for j in range(nodes):
        for k in range(1, groups):
            copy_a(j, k).wait_recv()
        for k in list(range(1, groups)) + [0]:
            value = arrived[j][map_ref[flip(me, k), col]]
            if k:
                send_b[j, k] = value
                copy_b(j, k).start()
            else:
                cur[0, j, 0] = value

    pieces = nodes * groups

    def place(t):
        late = t - nodes
        own = (t < nodes).astype(jnp.int32)
        rest = 1 - own
        return own * t + rest * (late // (groups - 1)), rest * (1 + late % (groups - 1))

    delays = [0] + [1 + 2 * level for level in range(last)]

    def sweep(t, carry):
        @pl.when(t < pieces)
        def _():
            j, k = place(t)

            @pl.when(t >= nodes)
            def _():
                copy_b(j, k).wait_recv()

            copy_x(0, j, k).start()

        for level in range(last):
            back = delays[level + 1]

            @pl.when(jnp.logical_and(t >= back, t < pieces + back))
            def _():
                j, k = place(t - back)
                copy_x(level, j, k).wait_recv()
                value = mm(transfer_ref[level, j, :, :rank], cur[level, j, k]) + mm(
                    far[level, j], got[level, j, k]
                )
                if level < last - 1:
                    cur[level + 1, j, k] = value
                    copy_x(level + 1, j, k).start()
                else:

                    @pl.when(t == back)
                    def _():
                        copy_w.wait_recv()

                    send_r[0, j, k] = mm(far_away[j], value)

                    @pl.when(k > 0)
                    def _():
                        copy_r(0, j, k).start()

                    send_r[1, j, k] = mm(transfer_ref[last, j, :, :rank], value)

                    @pl.when(k > 0)
                    def _():
                        copy_r(1, j, k).start()

        return carry

    lax.fori_loop(0, pieces + delays[-1], sweep, 0)

    for j in range(nodes):
        value = send_r[0, j, 0]
        for k in range(1, groups):
            copy_r(0, j, k).wait_recv()
            value = value + got_r[0, j, k]
        send_f[j] = value
        copy_f(j).start()
    for j in range(nodes):
        value = send_r[1, j, 0]
        for k in range(1, groups):
            copy_r(1, j, k).wait_recv()
            value = value + got_r[1, j, k]
        copy_f(j).wait_recv()
        value = value + got_f[j]
        out_ref[:, j * leaf : (j + 1) * leaf] = mm(value.T, src_ref[j], 1)

    copy_w.wait_send()

    def drain(step, carry):
        j = step // groups
        k = step % groups
        for level in range(last):
            copy_x(level, j, k).wait_send()

        @pl.when(k > 0)
        def _():
            remote(
                send_a.at[j, k], send_b.at[j, k], sem_a, (j, k), over_obs(k)
            ).wait_send()
            copy_b(j, k).wait_send()
            copy_r(0, j, k).wait_send()
            copy_r(1, j, k).wait_send()

        @pl.when(k == 0)
        def _():
            copy_f(j).wait_send()

        return carry

    lax.fori_loop(0, nodes * groups, drain, 0)


def body(obs_field, observer_leaf_bases, transfer, src_basis, leaf_map, partner_perm):
    nodes, leaf, rank = observer_leaf_bases.shape
    levels = transfer.shape[0]
    last = levels - 1
    groups = lax.axis_size("obs")
    share = obs_field.shape[1] // groups
    block = (nodes, groups, rank, share)

    def buffer(*shape):
        return pltpu.VMEM(shape, jnp.float32)

    vmem = pl.BlockSpec(memory_space=pltpu.VMEM)
    dma = pltpu.SemaphoreType.DMA
    return pl.pallas_call(
        functools.partial(kernel, groups),
        out_shape=jax.ShapeDtypeStruct((share, nodes * leaf), jnp.float32),
        in_specs=[vmem] * 5 + [pl.BlockSpec(memory_space=pltpu.SMEM)],
        out_specs=vmem,
        scratch_shapes=[
            buffer(nodes, rank, leaf),
            buffer(levels, nodes, rank, rank),
            buffer(nodes, rank, rank),
            buffer(*block),
            buffer(*block),
            buffer(last, *block),
            buffer(last, *block),
            buffer(2, *block),
            buffer(2, *block),
            buffer(nodes, rank, share),
            buffer(nodes, rank, share),
            dma((2, 1)),
            dma((2, nodes, groups)),
            dma((2, nodes, groups)),
            dma((2, last, nodes, groups)),
            dma((2, 2, nodes, groups)),
            dma((2, nodes)),
        ]
        + [buffer(groups, rank, share)] * nodes,
        compiler_params=pltpu.CompilerParams(collective_id=0, has_side_effects=True),
    )(
        obs_field,
        observer_leaf_bases,
        transfer,
        src_basis,
        partner_perm.reshape(levels, 1, rank),
        leaf_map,
    )


def solution(mesh):
    placed = (
        P(("obs", "bfly"), None),
        P(("obs", "bfly"), None, None),
        P(None, ("obs", "bfly"), None, None),
        P("bfly", None, None),
        P(),
        P(),
    )
    return jax.shard_map(
        body, mesh=mesh, in_specs=placed, out_specs=P("obs", "bfly"), check_vma=False
    )
```

profile of v0, /device:TPU:0, one launch (start us, length us, event | category | flops | bytes accessed | tf_op | source)
XLA Modules:
  0.0 119.2 jit_solution(7320846747956212907)
XLA Ops:
  0.0 1.3 %reshape.3.perm_ref = s32[3,1,256]{2,1,0:T(1,128)} reshape(s32[3,256]{1,0:T(4,128)} %param.11) | data formatting | bytes 6144 | tf_op jit(solution)/shard_map/reshape | solution.py:302
  1.3 115.6 %shard_map.64 = f32[256,1024]{1,0:T(8,128)} custom-call(f32[1024,1024]{1,0:T(8,128)} %obs_ref.1, f32[2,512,256]{2,1,0:T(8,128)} %bases_ref.1, f32[3,2,256,512]{3,2,1,0:T(8,128)} %transfer_ref.1, f32[2,512,256]{2,1,0:T(8,128)} %src_ref.1, s32[3,1,256]{2,1,0:T(1,128)} %reshape.3.perm_ref, s32[4,8]{1,0:T(4,128)} %map_ref.1), custom_call_target="tpu_custom_call" | custom-call | tf_op jit(solution)/shard_map/pallas_call | solution.py:271
  116.9 2.3 %copy.8 = f32[256,1024]{1,0:T(8,128)} copy(f32[256,1024]{1,0:T(8,128)} %shard_map.64) | data formatting | bytes 2097152
where the time goes:
time: 119 us
  Pallas kernels  116 us (97%)
  local copies, waits for them, and re-layouts  3.57 us (3%)
    pallas_call x1, Pallas kernels, body(): pl.pallas_call(functools.partial(kernel, groups), out_shape=jax.ShapeDtyp...  116 us

commit v1 on v0

--- a/solution.py
+++ b/solution.py
@@ -92,9 +92,22 @@
             cur.at[level, j, k], got.at[level, j, k], sem_x, (level, j, k), over_bfly(level)
         )
 
+    bits = [1 << i for i in range((groups - 1).bit_length())]
+    hops, donors = [], []
+    for ladder in (bits, bits[::-1]):
+        hop = {k: next(bit for bit in ladder if k & bit) for k in range(1, groups)}
+        hops.append(hop)
+        donors.append(
+            [[k for k in hop if k ^ hop[k] == chunk] for chunk in range(groups)]
+        )
+
     def copy_r(which, j, k):
         return remote(
-            send_r.at[which, j, k], got_r.at[which, j, k], sem_r, (which, j, k), over_obs(k)
+            send_r.at[which, j, k],
+            got_r.at[which, j, k],
+            sem_r,
+            (which, j, k),
+            over_obs(hops[which][k]),
         )
 
     def copy_f(j):
@@ -132,24 +145,23 @@
     for j in range(nodes):
         lax.fori_loop(0, groups, functools.partial(project, j), 0)
 
-    def fold(step, carry):
-        level = last - step // nodes
-        j = step % nodes
-        hot = lax.broadcasted_iota(jnp.int32, (rank, rank), 0) == perm_ref[level]
-        far[level, j] = mm(transfer_ref[level, j, :, rank:], hot.astype(jnp.float32), 1)
-
-        @pl.when(step == nodes - 1)
-        def _():
+    def fold(level, hot, j, carry):
+        far[level, j] = mm(transfer_ref[level, j, :, rank:], hot, 1)
+        return carry
+
+    for level in range(last, -1, -1):
+        rows = lax.broadcasted_iota(jnp.int32, (rank, rank), 0)
+        hot = (rows == perm_ref[level : level + 1, :]).astype(jnp.float32)
+        lax.fori_loop(0, nodes, functools.partial(fold, level, hot), 0)
+        if level == last:
             copy_w.start()
 
-        return carry
-
-    lax.fori_loop(0, levels * nodes, fold, 0)
-
-    for j in range(nodes):
-        for k in range(1, groups):
+    order = list(range(groups - 1, groups - 2, -1)) + list(range(1, groups - 1))
+
+    def pick(j):
+        for k in order:
             copy_a(j, k).wait_recv()
-        for k in list(range(1, groups)) + [0]:
+        for k in order + [0]:
             value = arrived[j][map_ref[flip(me, k), col]]
             if k:
                 send_b[j, k] = value
@@ -163,68 +175,109 @@
         late = t - nodes
         own = (t < nodes).astype(jnp.int32)
         rest = 1 - own
-        return own * t + rest * (late // (groups - 1)), rest * (1 + late % (groups - 1))
-
-    delays = [0] + [1 + 2 * level for level in range(last)]
+        turn = late % (groups - 1)
+        return (
+            own * t + rest * (late // (groups - 1)),
+            rest * (turn + (groups - 1) * (turn == 0).astype(jnp.int32)),
+        )
+
+    level_back = [1 + 2 * level for level in range(last)]
+    far_back = level_back[-1]
+    backs = (far_back, far_back + 3)
+
+    def active(t, back):
+        return jnp.logical_and(t >= back, t < pieces + back)
+
+    def send_part(which, t):
+        j, k = place(t)
+        weights = far_away[j] if which == 0 else transfer_ref[last, j, :, :rank]
+        send_r[which, j, k] = mm(weights, cur[last, j, k])
 
     def sweep(t, carry):
-        @pl.when(t < pieces)
-        def _():
-            j, k = place(t)
-
-            @pl.when(t >= nodes)
-            def _():
-                copy_b(j, k).wait_recv()
-
-            copy_x(0, j, k).start()
-
         for level in range(last):
-            back = delays[level + 1]
-
-            @pl.when(jnp.logical_and(t >= back, t < pieces + back))
-            def _():
-                j, k = place(t - back)
+
+            @pl.when(active(t, level_back[level]))
+            def _():
+                j, k = place(t - level_back[level])
                 copy_x(level, j, k).wait_recv()
                 value = mm(transfer_ref[level, j, :, :rank], cur[level, j, k]) + mm(
                     far[level, j], got[level, j, k]
                 )
+                cur[level + 1, j, k] = value
                 if level < last - 1:
-                    cur[level + 1, j, k] = value
                     copy_x(level + 1, j, k).start()
                 else:
 
-                    @pl.when(t == back)
+                    @pl.when(t == far_back)
                     def _():
                         copy_w.wait_recv()
 
-                    send_r[0, j, k] = mm(far_away[j], value)
-
-                    @pl.when(k > 0)
+            if level == 0:
+                for j in range(nodes):
+
+                    @pl.when(t == j)
                     def _():
-                        copy_r(0, j, k).start()
-
-                    send_r[1, j, k] = mm(transfer_ref[last, j, :, :rank], value)
-
-                    @pl.when(k > 0)
+                        pick(j)
+
+                @pl.when(t < pieces)
+                def _():
+                    j, k = place(t)
+
+                    @pl.when(t >= nodes)
                     def _():
-                        copy_r(1, j, k).start()
+                        copy_b(j, k).wait_recv()
+
+                    copy_x(0, j, k).start()
+
+        for which in range(2):
+            back = backs[which]
+
+            @pl.when(active(t, back))
+            def _():
+                send_part(which, t - back)
+
+            @pl.when(active(t, back))
+            def _():
+                j, k = place(t - back)
+
+                @pl.when(k > 0)
+                def _():
+                    for chunk in range(1, groups):
+                        if not donors[which][chunk]:
+
+                            @pl.when(k == chunk)
+                            def _():
+                                copy_r(which, j, chunk).start()
+
+            @pl.when(active(t, back + 1))
+            def _():
+                j, k = place(t - back - 1)
+                for chunk in range(1, groups):
+                    if donors[which][chunk]:
+
+                        @pl.when(k == chunk)
+                        def _():
+                            for donor in donors[which][chunk]:
+                                copy_r(which, j, donor).wait_recv()
+                                send_r[which, j, chunk] += got_r[which, j, donor]
+                            copy_r(which, j, chunk).start()
 
         return carry
 
-    lax.fori_loop(0, pieces + delays[-1], sweep, 0)
+    lax.fori_loop(0, pieces + backs[1] + 1, sweep, 0)
 
     for j in range(nodes):
         value = send_r[0, j, 0]
-        for k in range(1, groups):
-            copy_r(0, j, k).wait_recv()
-            value = value + got_r[0, j, k]
+        for donor in donors[0][0]:
+            copy_r(0, j, donor).wait_recv()
+            value = value + got_r[0, j, donor]
         send_f[j] = value
         copy_f(j).start()
     for j in range(nodes):
         value = send_r[1, j, 0]
-        for k in range(1, groups):
-            copy_r(1, j, k).wait_recv()
-            value = value + got_r[1, j, k]
+        for donor in donors[1][0]:
+            copy_r(1, j, donor).wait_recv()
+            value = value + got_r[1, j, donor]
         copy_f(j).wait_recv()
         value = value + got_f[j]
         out_ref[:, j * leaf : (j + 1) * leaf] = mm(value.T, src_ref[j], 1)
@@ -243,8 +296,13 @@
                 send_a.at[j, k], send_b.at[j, k], sem_a, (j, k), over_obs(k)
             ).wait_send()
             copy_b(j, k).wait_send()
-            copy_r(0, j, k).wait_send()
-            copy_r(1, j, k).wait_send()
+
+        for chunk in range(1, groups):
+
+            @pl.when(k == chunk)
+            def _():
+                for which in range(2):
+                    copy_r(which, j, chunk).wait_send()
 
         @pl.when(k == 0)
         def _():
@@ -279,7 +337,7 @@
             buffer(nodes, rank, rank),
             buffer(*block),
             buffer(*block),
-            buffer(last, *block),
+            buffer(last + 1, *block),
             buffer(last, *block),
             buffer(2, *block),
             buffer(2, *block),
@@ -299,7 +357,7 @@
         observer_leaf_bases,
         transfer,
         src_basis,
-        partner_perm.reshape(levels, 1, rank),
+        partner_perm,
         leaf_map,
     )
 

time: 119 us -> 129 us (1.084)
  Pallas kernels: 116 us -> 127 us
    pallas_call x1, Pallas kernels: 116 us -> 127 us  [body(): pl.pallas_call(functools.partial(kernel, groups), out_shape=jax.ShapeDtyp...]
where the time goes in v1:
time: 129 us
  Pallas kernels  127 us (98%)
  local copies, waits for them, and re-layouts  2.31 us (2%)
    pallas_call x1, Pallas kernels, body(): pl.pallas_call(functools.partial(kernel, groups), out_shape=jax.ShapeDtyp...  127 us

profile of v1, /device:TPU:0, one launch (start us, length us, event | category | flops | bytes accessed | tf_op | source)
XLA Modules:
  0.0 129.1 jit_solution(12059126675248879006)
XLA Ops:
  0.0 126.8 %shard_map.64 = f32[256,1024]{1,0:T(8,128)} custom-call(f32[1024,1024]{1,0:T(8,128)} %obs_ref.1, f32[2,512,256]{2,1,0:T(8,128)} %bases_ref.1, f32[3,2,256,512]{3,2,1,0:T(8,128)} %transfer_ref.1, f32[2,512,256]{2,1,0:T(8,128)} %src_ref.1, s32[3,256]{1,0:T(4,128)} %perm_ref.1, s32[4,8]{1,0:T(4,128)} %map_ref.1), custom_call_target="tpu_custom_call" | custom-call | tf_op jit(solution)/shard_map/pallas_call | solution.py:329
  126.8 2.3 %copy.8 = f32[256,1024]{1,0:T(8,128)} copy(f32[256,1024]{1,0:T(8,128)} %shard_map.64) | data formatting | bytes 2097152

commit v2 on v1

--- a/solution.py
+++ b/solution.py
@@ -181,9 +181,9 @@
             rest * (turn + (groups - 1) * (turn == 0).astype(jnp.int32)),
         )
 
-    level_back = [1 + 2 * level for level in range(last)]
+    level_back = [1 + 3 * level for level in range(last)]
     far_back = level_back[-1]
-    backs = (far_back, far_back + 3)
+    backs = (far_back, far_back)
 
     def active(t, back):
         return jnp.logical_and(t >= back, t < pieces + back)

time: 129 us -> 113 us (0.88)
  Pallas kernels: 127 us -> 110 us
    pallas_call x1, Pallas kernels: 127 us -> 110 us  [body(): pl.pallas_call(functools.partial(kernel, groups), out_shape=jax.ShapeDtyp...]
where the time goes in v2:
time: 113 us
  Pallas kernels  110 us (97%)
  local copies, waits for them, and re-layouts  2.31 us (2%)
    pallas_call x1, Pallas kernels, body(): pl.pallas_call(functools.partial(kernel, groups), out_shape=jax.ShapeDtyp...  110 us
    unnamed x1, local copies, waits for them, and re-layouts  2.31 us

profile of v2, /device:TPU:0, one launch (start us, length us, event | category | flops | bytes accessed | tf_op | source)
XLA Modules:
  0.0 112.5 jit_solution(15519902622672524345)
XLA Ops:
  0.0 110.2 %shard_map.64 = f32[256,1024]{1,0:T(8,128)} custom-call(f32[1024,1024]{1,0:T(8,128)} %obs_ref.1, f32[2,512,256]{2,1,0:T(8,128)} %bases_ref.1, f32[3,2,256,512]{3,2,1,0:T(8,128)} %transfer_ref.1, f32[2,512,256]{2,1,0:T(8,128)} %src_ref.1, s32[3,256]{1,0:T(4,128)} %perm_ref.1, s32[4,8]{1,0:T(4,128)} %map_ref.1), custom_call_target="tpu_custom_call" | custom-call | tf_op jit(solution)/shard_map/pallas_call | solution.py:329
  110.2 2.3 %copy.8 = f32[256,1024]{1,0:T(8,128)} copy(f32[256,1024]{1,0:T(8,128)} %shard_map.64) | data formatting | bytes 2097152
